TPU v7x, 32 devices: a whole 2x2x4 slice. The times are simulated.
32 devices in a mesh: cam: 4 (over x, core), pt: 8 (over z, y).
Axes of the slice: x: 2, y: 2, z: 4, core: 2. Of those that a mesh axis runs over, the one named last changes fastest.
Arguments:
- right_side: float32 [9, 65536], P(None, ('cam', 'pt')), may hold values from -6 to 6
- cam_damping: float32 [9, 65536], P(None, ('cam', 'pt')), may hold values from 0.5 to 4
- point_damping: float32 [524288], P('pt'), may hold values from 0.1 to 1
- block_ids: int32 [4, 8, 64], P('cam', 'pt'), may hold values from 0 to 255, as said below
- slab_ids: int32 [4, 8, 64], P('cam', 'pt'), may hold values from 0 to 15
- cam_index: int32 [4, 8, 64, 4096], P('cam', 'pt'), may hold values from 0 to 63
- cam_jacobian: bfloat16 [4, 8, 64, 18, 4096], P('cam', 'pt'), may hold values from -0.59765625 to 0.59765625
- point_jacobian: bfloat16 [4, 8, 64, 6, 4096], P('cam', 'pt'), may hold values from -1.796875 to 1.796875
- pair_count: int32 [4, 8], P('cam', 'pt'), may hold values from 16 to 64, as said below
Outputs:
- solution: float32 [9, 65536], P(None, ('cam', 'pt'))
- residual: float32 [9, 65536], P(None, ('cam', 'pt'))
Inputs may be any that keep to these rules, and one draw needn't show every extreme that they name: pair_count is 64 divided by a whole number from 1 to 4, rounded down; at least one device has all 64 slots used in every draw. The owner of a block is block_ids // 32; in every device's list at most 16 slots name blocks of one owner, and in every list some owner is named by exactly 16 slots.
All inputs are finite; a program needn't handle non-finite values.
Results may differ from a plain program's by a relative error of at most 0.0003.
Values sent between devices are 32-bit elements; how exact they have to be, the bound alone decides.
A program may use at most 128 MiB of HBM per device.

v0:
```python
import jax
import jax.numpy as jnp
from jax import lax
from jax.sharding import PartitionSpec as P

BLOCK = 64
ITERS = 2


HIGH = lax.Precision.HIGHEST


def hessian_terms(pt_jac):
    combos = [(0, 0), (0, 1), (0, 2), (1, 1), (1, 2), (2, 2)]
    return jnp.stack(
        [
            jnp.sum(pt_jac[:, :, first].astype(jnp.float32) * pt_jac[:, :, second], axis=1)
            for first, second in combos
        ],
        axis=1,
    )


def collect(selector, terms):
    summed = jnp.einsum("ps,pkn->ksn", selector, terms, precision=HIGH)
    return summed.reshape(terms.shape[1], -1)


def invert_points(hess, damping):
    entry_xx = hess[0] + damping
    entry_xy = hess[1]
    entry_xz = hess[2]
    entry_yy = hess[3] + damping
    entry_yz = hess[4]
    entry_zz = hess[5] + damping
    cof_xx = entry_yy * entry_zz - entry_yz * entry_yz
    cof_xy = entry_xz * entry_yz - entry_xy * entry_zz
    cof_xz = entry_xy * entry_yz - entry_xz * entry_yy
    cof_yy = entry_xx * entry_zz - entry_xz * entry_xz
    cof_yz = entry_xy * entry_xz - entry_xx * entry_yz
    cof_zz = entry_xx * entry_yy - entry_xy * entry_xy
    determinant = entry_xx * cof_xx + entry_xy * cof_xy + entry_xz * cof_xz
    return jnp.stack([cof_xx, cof_xy, cof_xz, cof_yy, cof_yz, cof_zz]) / determinant


def apply_inverse(inverse, vector):
    out_x = inverse[0] * vector[0] + inverse[1] * vector[1] + inverse[2] * vector[2]
    out_y = inverse[1] * vector[0] + inverse[3] * vector[1] + inverse[4] * vector[2]
    out_z = inverse[2] * vector[0] + inverse[4] * vector[1] + inverse[5] * vector[2]
    return jnp.stack([out_x, out_y, out_z])


def select_cameras(picked, index_here):
    pairs = picked.shape[0]

    def select_per_group(pieces):
        picked_group, index_group = pieces
        one_hot = (
            index_group[:, :, None] == jnp.arange(BLOCK, dtype=jnp.int32)[None, None, :]
        ).astype(jnp.float32)
        return jnp.einsum("gkb,gnb->gkn", picked_group, one_hot, precision=HIGH)

    grouped = lax.map(
        select_per_group,
        (picked.reshape(pairs // 8, 8, 9, BLOCK), index_here.reshape(pairs // 8, 8, -1)),
    )
    return grouped.reshape(pairs, 9, -1)


def project(cam_panel, blocks_here, index_here, cam_jac):
    grouped = cam_panel.reshape(9, -1, BLOCK).transpose(1, 0, 2)
    picked = grouped[blocks_here]
    at_camera = select_cameras(picked, index_here)
    return jnp.sum(cam_jac * at_camera[:, None], axis=2)


def camera_sums(pushed, index_here):
    pairs = pushed.shape[0]

    def camera_per_group(pieces):
        pushed_group, index_group = pieces
        one_hot = (
            index_group[:, :, None] == jnp.arange(BLOCK, dtype=jnp.int32)[None, None, :]
        ).astype(jnp.float32)
        return jnp.einsum("gkn,gnb->gkb", pushed_group, one_hot, precision=HIGH)

    grouped = lax.map(
        camera_per_group,
        (pushed.reshape(pairs // 8, 8, 9, -1), index_here.reshape(pairs // 8, 8, -1)),
    )
    return grouped.reshape(pairs, 9, BLOCK)


def dot_whole(first, second):
    return lax.psum(jnp.sum(first * second), "cam")


def per_device(
    right_side,
    cam_damping,
    point_damping,
    block_ids,
    slab_ids,
    cam_index,
    cam_jacobian,
    point_jacobian,
    pair_count,
):
    pairs = block_ids.shape[2]
    slab_len = cam_index.shape[3]
    slabs = point_damping.shape[0] // slab_len
    cam_dev = right_side.shape[1]
    owners_count = lax.axis_size("pt")
    blk_owner = cam_dev // BLOCK
    blk_group = blk_owner * owners_count
    blocks_here = block_ids.reshape(pairs)
    slabs_here = slab_ids.reshape(pairs)
    index_here = cam_index.reshape(pairs, slab_len)
    cam_jac = cam_jacobian.reshape(pairs, 2, 9, slab_len)
    pt_jac = point_jacobian.reshape(pairs, 2, 3, slab_len)
    live_pairs = (jnp.arange(pairs, dtype=jnp.int32) < pair_count.reshape(())).astype(jnp.float32)
    slab_onehot = (slabs_here[:, None] == jnp.arange(slabs, dtype=jnp.int32)[None, :]).astype(
        jnp.float32
    )
    selector = slab_onehot * live_pairs[:, None]
    block_onehot = (blocks_here[:, None] == jnp.arange(blk_group, dtype=jnp.int32)[None, :]).astype(
        jnp.float32
    )
    hess_local = collect(selector, hessian_terms(pt_jac))
    inverse = invert_points(lax.psum(hess_local, "cam"), point_damping)
    residual, damping_here = (
        lax.all_gather(right_side, "pt", axis=1, tiled=True),
        lax.all_gather(cam_damping, "pt", axis=1, tiled=True),
    )
    solution = jnp.zeros_like(residual)
    direction = residual
    norm_now = dot_whole(residual, residual)
    for iteration in range(ITERS):
        projected = project(direction, blocks_here, index_here, cam_jac)
        pulled = jnp.sum(pt_jac * projected[:, :, None], axis=1)
        eliminated = apply_inverse(inverse, lax.psum(collect(selector, pulled), "cam")).reshape(
            3, slabs, slab_len
        )
        pulled_back = jnp.einsum("ps,ksn->pkn", slab_onehot, eliminated, precision=HIGH)
        miss = projected - jnp.sum(pt_jac * pulled_back[:, None], axis=2)
        pushed = jnp.sum(cam_jac * miss[:, :, None], axis=1)
        group_sum = jnp.einsum(
            "pg,pkb->kgb",
            block_onehot,
            camera_sums(pushed, index_here) * live_pairs[:, None, None],
            precision=HIGH,
        )
        image = damping_here * direction + lax.psum(group_sum.reshape(9, blk_group * BLOCK), "pt")
        step_size = norm_now / dot_whole(direction, image)
        solution = solution + step_size * direction
        residual = residual - step_size * image
        norm_next = dot_whole(residual, residual)
        direction = residual + norm_next / norm_now * direction
        norm_now = norm_next
    start = lax.axis_index("pt") * cam_dev
    solution = lax.dynamic_slice_in_dim(solution, start, cam_dev, 1)
    residual = lax.dynamic_slice_in_dim(residual, start, cam_dev, 1)
    return (solution, residual)


def solution(mesh):
    in_specs = (
        P(None, ("cam", "pt")),
        P(None, ("cam", "pt")),
        P("pt"),
        P("cam", "pt", None),
        P("cam", "pt", None),
        P("cam", "pt", None, None),
        P("cam", "pt", None, None, None),
        P("cam", "pt", None, None, None),
        P("cam", "pt"),
    )
    out_specs = (P(None, ("cam", "pt")), P(None, ("cam", "pt")))
    return jax.shard_map(
        per_device, mesh=mesh, in_specs=in_specs, out_specs=out_specs, check_vma=False
    )
```

profile of v0, /device:TPU:0, one launch (start us, length us, event | category | flops | bytes accessed | tf_op | source)
XLA Modules:
  0.0 737.0 jit_solution(18072257541709590716)
XLA Ops:
  18.2 34.7 %all_gather.6 = f32[9,16384]{1,0:T(8,128)S(1)} all-gather(f32[9,2048]{1,0:T(8,128)S(1)} %copy-done.11), channel_id=1, replica_groups=mesh['cam'=4,'pt'=8] {'pt'}, dimensions={1}, use_global_device_ids=true | all-gather | bytes 663552 | tf_op jit(solution)/shard_map/all_gather | solution.py:132
  57.7 7.8 %broadcast.107.clone = f32[8,8,9,4096]{3,2,1,0:T(8,128)} broadcast(f32[]{:T(128)} %constant.49.clone.1), dimensions={} | broadcast | bytes 9437188 | tf_op jit(solution)/shard_map/broadcast.5
  65.6 39.4 %while.40 = (s32[]{:T(128)}, f32[8,8,9,4096]{3,2,1,0:T(8,128)}, f32[8,8,9,64]{3,2,1,0:T(8,128)S(1)}, s32[8,8,4096]{2,1,0:T(8,128)}, s32[]{:T(128)}) while((s32[]{:T(128)}, f32[8,8,9,4096]{3,2,1,0:T(8,128)}, f32[8,8,9,64]{3,2,1,0:T(8,128)S(1)}, s32[8,8,4096]{2,1,0:T(8,128)}, s32[]{:T(128)}) %tuple.115), condition=%wide.region_3.0_spmd, body=%wide.region_2.0_spmd.sunk | while | flops 228589568 | bytes 2556993 | solution.py:63
  104.9 14.9 %copy.26 = f32[64,9,4096]{2,0,1:T(8,128)} copy(f32[64,9,4096]{2,1,0:T(8,128)} %bitcast.161) | data formatting | bytes 18874368 | tf_op jit(solution)/shard_map/mul | solution.py:74
  119.8 8.0 %fusion.22 = f32[64,2,4096]{2,0,1:T(8,128)S(1)} fusion(bf16[64,2,9,4096]{3,0,2,1:T(8,128)(2,1)} %bitcast.152, f32[64,9,4096]{2,0,1:T(8,128)} %copy.26), kind=kLoop, calls=%fused_computation.40 | loop fusion | flops 13631488 | bytes 20971520 | tf_op jit(solution)/shard_map/reduce_sum | solution.py:74
  132.5 69.4 %all-reduce.13.cloned.1.call-done = (f32[6,65536]{1,0:T(8,128)}, f32[3,65536]{1,0:T(4,128)}) async-done(((f32[6,65536]{1,0:T(8,128)}, f32[3,65536]{1,0:T(4,128)}), (f32[6,65536]{1,0:T(8,128)}, f32[3,65536]{1,0:T(4,128)})) %all-reduce.13.cloned.1.call-update) | async-done | bytes 2359312 | tf_op jit(solution)/shard_map/psum | solution.py:130
  201.9 6.8 fusion.84
  211.5 6.5 stack.79
  235.7 11.2 %fusion.23 = f32[64,9,4096]{2,0,1:T(8,128)} fusion(bf16[64,2,9,4096]{3,0,2,1:T(8,128)(2,1)} %bitcast.153, f32[64,2,4096]{2,0,1:T(8,128)} %sub.44), kind=kLoop, calls=%fused_computation.41 | loop fusion | flops 11796480 | bytes 20971520 | tf_op jit(solution)/shard_map/reduce_sum | solution.py:146
  247.7 58.1 %while.41 = (s32[]{:T(128)}, f32[8,8,9,64]{3,2,1,0:T(8,128)}, f32[8,8,9,4096]{3,1,0,2:T(8,128)}, s32[8,8,4096]{2,1,0:T(8,128)}, s32[]{:T(128)}) while((s32[]{:T(128)}, f32[8,8,9,64]{3,2,1,0:T(8,128)}, f32[8,8,9,4096]{3,1,0,2:T(8,128)}, s32[8,8,4096]{2,1,0:T(8,128)}, s32[]{:T(128)}) %tuple.111), condition=%wide.region_17.18_spmd, body=%wide.region_16.17_spmd.sunk | while | flops 228589568 | bytes 3998277 | solution.py:87
  313.7 36.7 %all_gather.7 = f32[9,16384]{1,0:T(8,128)} all-gather(f32[9,2048]{1,0:T(8,128)S(1)} %copy-done.12), channel_id=1, replica_groups=mesh['cam'=4,'pt'=8] {'pt'}, dimensions={1}, use_global_device_ids=true | all-gather | bytes 663552 | tf_op jit(solution)/shard_map/all_gather | solution.py:133
  350.4 49.2 %all-reduce.7.cloned.1.call-done = f32[9,16384]{1,0:T(8,128)} async-done(((f32[9,16384]{1,0:T(8,128)}), f32[9,16384]{1,0:T(8,128)}) %all-reduce.7.cloned.1.call-update) | async-done | bytes 589840 | tf_op jit(solution)/shard_map/psum | solution.py:153
  402.3 7.1 all-reduce
  414.5 6.6 psum.68
  434.1 7.8 %broadcast.107 = f32[8,8,9,4096]{3,2,1,0:T(8,128)} broadcast(f32[]{:T(128)} %constant.49.clone.1), dimensions={} | broadcast | bytes 9437188 | tf_op jit(solution)/shard_map/broadcast.5
  441.9 45.9 %while.42 = (s32[]{:T(128)}, f32[8,8,9,4096]{3,2,1,0:T(8,128)}, f32[8,8,9,64]{3,2,1,0:T(8,128)}, s32[8,8,4096]{2,1,0:T(8,128)}, s32[]{:T(128)}) while((s32[]{:T(128)}, f32[8,8,9,4096]{3,2,1,0:T(8,128)}, f32[8,8,9,64]{3,2,1,0:T(8,128)}, s32[8,8,4096]{2,1,0:T(8,128)}, s32[]{:T(128)}) %tuple.114), condition=%wide.region_24.25_spmd, body=%wide.region_23.24_spmd.sunk | while | flops 228589568 | bytes 2556993 | solution.py:63
  487.8 14.9 %copy.31 = f32[64,9,4096]{2,0,1:T(8,128)} copy(f32[64,9,4096]{2,1,0:T(8,128)} %bitcast.162) | data formatting | bytes 18874368 | tf_op jit(solution)/shard_map/mul | solution.py:74
  502.6 7.6 %fusion.24 = f32[64,2,4096]{2,0,1:T(8,128)S(1)} fusion(bf16[64,2,9,4096]{3,0,2,1:T(8,128)(2,1)} %bitcast.154, f32[64,9,4096]{2,0,1:T(8,128)} %copy.31), kind=kLoop, calls=%fused_computation.42 | loop fusion | flops 13631488 | bytes 20971520 | tf_op jit(solution)/shard_map/reduce_sum | solution.py:74
  514.9 35.6 %all-reduce.9.cloned.1.call-done = f32[3,65536]{1,0:T(4,128)} async-done(((f32[3,65536]{1,0:T(4,128)}), f32[3,65536]{1,0:T(4,128)}) %all-reduce.9.cloned.1.call-update) | async-done | bytes 786448 | tf_op jit(solution)/shard_map/psum | solution.py:141
  550.5 11.2 %add_reduce_fusion.2 = (f32[65536]{0:T(1024)}, f32[65536]{0:T(1024)}, f32[65536]{0:T(1024)S(1)}) fusion(f32[6,65536]{1,0:T(8,128)} %copy-done.7, f32[3,65536]{1,0:T(4,128)} %all-reduce.9.cloned.1.call-done), kind=kLoop, calls=%fused_computation.102 | loop fusion | flops 983040 | bytes 3145728 | tf_op jit(solution)/shard_map/add | solution.py:47
  570.2 10.6 %fusion.25 = f32[64,9,4096]{2,0,1:T(8,128)} fusion(bf16[64,2,9,4096]{3,0,2,1:T(8,128)(2,1)} %bitcast.155, f32[64,2,4096]{2,0,1:T(8,128)S(1)} %sub.46), kind=kLoop, calls=%fused_computation.43 | loop fusion | flops 11796480 | bytes 20971520 | tf_op jit(solution)/shard_map/reduce_sum | solution.py:146
  580.9 53.1 %while.43 = (s32[]{:T(128)}, f32[8,8,9,64]{3,2,1,0:T(8,128)S(1)}, f32[8,8,9,4096]{3,1,0,2:T(8,128)}, s32[8,8,4096]{2,1,0:T(8,128)}, s32[]{:T(128)}) while((s32[]{:T(128)}, f32[8,8,9,64]{3,2,1,0:T(8,128)S(1)}, f32[8,8,9,4096]{3,1,0,2:T(8,128)}, s32[8,8,4096]{2,1,0:T(8,128)}, s32[]{:T(128)}) %tuple.113), condition=%wide.region_31.32_spmd, body=%wide.region_30.31_spmd.sunk | while | flops 228589568 | bytes 3997769 | solution.py:87
  638.8 79.0 %all-reduce.11.cloned.1.call-done = f32[9,16384]{1,0:T(8,128)} async-done(((f32[9,16384]{1,0:T(8,128)}), f32[9,16384]{1,0:T(8,128)}) %all-reduce.11.cloned.1.call-update) | async-done | bytes 589840 | tf_op jit(solution)/shard_map/psum | solution.py:153
  719.9 7.1 psum.71
  (173 shorter events, 284.9 us)
Async XLA Ops:
  7.2 194.7 %all-reduce.13.cloned.1.call-start = ((), (), s32[]{:S(2)}) async-start(), calls=%async_computation.3 | async-start | bytes 6291456 | tf_op jit(solution)/shard_map/psum | solution.py:130
  11.9 0.7 copy-start.13
  16.0 2.3 copy-start.11
  18.2 37.3 %copy-start.14 = (s32[1,1,64]{2,1,0:T(1,128)S(1)}, s32[1,1,64]{2,1,0:T(1,128)}, u32[]{:S(2)}) copy-start(s32[1,1,64]{2,1,0:T(1,128)} %param.20) | copy-start | bytes 772
  53.0 4.8 copy-start.1
  119.8 8.0 %copy-start = (bf16[1,1,64,6,4096]{4,2,3,1,0:T(8,128)(2,1)S(1)}, bf16[1,1,64,6,4096]{4,2,3,1,0:T(8,128)(2,1)}, u32[]{:S(2)}) copy-start(bf16[1,1,64,6,4096]{4,2,3,1,0:T(8,128)(2,1)} %param.24) | copy-start | bytes 9437188
  127.8 1.4 copy-start.2
  132.5 267.1 %all-reduce.7.cloned.1.call-start = ((), (), s32[]{:S(2)}) async-start(), calls=%async_computation | async-start | bytes 2097152 | tf_op jit(solution)/shard_map/psum | solution.py:153
  201.9 8.7 %copy-start.9 = (f32[65536]{0:T(1024)S(1)}, f32[65536]{0:T(1024)}, u32[]{:S(2)}) copy-start(f32[65536]{0:T(1024)} %param.19) | copy-start | bytes 786436
  218.0 3.3 copy-start.10
  220.0 1.3 copy-start.7
  232.6 1.6 copy-start.3
  308.4 5.3 copy-start.12
  313.6 236.8 %all-reduce.9.cloned.1.call-start = ((), (), s32[]{:S(2)}) async-start(), calls=%async_computation.1 | async-start | bytes 2097152 | tf_op jit(solution)/shard_map/psum | solution.py:141
  510.2 1.4 copy-start.4
  514.9 202.9 %all-reduce.11.cloned.1.call-start = ((), (), s32[]{:S(2)}) async-start(), calls=%async_computation.2 | async-start | bytes 2097152 | tf_op jit(solution)/shard_map/psum | solution.py:153
  568.4 1.6 copy-start.5
  634.2 83.6 %copy-start.6 = (f32[9,16384]{1,0:T(8,128)S(1)}, f32[9,16384]{1,0:T(8,128)}, u32[]{:S(2)}) copy-start(f32[9,16384]{1,0:T(8,128)} %all_gather.7) | copy-start | bytes 1769476
  634.2 83.6 %copy-start.8 = (f32[9,16384]{1,0:T(8,128)S(1)}, f32[9,16384]{1,0:T(8,128)}, u32[]{:S(2)}) copy-start(f32[9,16384]{1,0:T(8,128)} %multiply_add_fusion.1) | copy-start | bytes 1769476
Sparse Core Ops, SparseCore 0:
  132.6 69.2 all-reduce.12
  313.8 85.7 all-reduce.6
  515.0 35.4 all-reduce.8
  638.9 78.8 all-reduce.10
where the time goes:
time: 747 us; the launch traced here: 737 us
  waiting for transfers between devices  233 us (31%)
  matrix products  159 us (21%)
  local copies, waits for them, and re-layouts  153 us (20%)
  blocking collectives  92.2 us (12%)
  other arithmetic  79.7 us (11%)
  between operations  19.2 us (3%)
    psum x2, waiting for transfers between devices, per_device(): lax.psum(group_sum.reshape(9, blk_group * BLOCK), 'pt')  128 us
    dot_general x16, matrix products, camera_per_group(): return jnp.einsum('gkn,gnb->gkb', pushed_group, one_hot, precision=HIGH)  74.6 us
    dot_general x16, matrix products, select_per_group(): return jnp.einsum('gkb,gnb->gkn', picked_group, one_hot, precision=HIGH)  70.4 us
    psum x1, waiting for transfers between devices, per_device(): inverse = invert_points(lax.psum(hess_local, 'cam'), point_damping)  69.4 us
    all_gather x1, blocking collectives, per_device(): lax.all_gather(cam_damping, 'pt', axis=1, tiled=True)  36.7 us
    psum x1, waiting for transfers between devices, per_device(): lax.psum(collect(selector, pulled), 'cam')  35.6 us
    all_gather x1, blocking collectives, per_device(): lax.all_gather(right_side, 'pt', axis=1, tiled=True)  34.7 us
    mul x2, local copies, waits for them, and re-layouts, project(): return jnp.sum(cam_jac * at_camera[:, None], axis=2)  29.7 us
  transfers between devices with their start and end apart: 4, of which 4 were waited for; matrix products, arithmetic and copies ran while one was open for 0% of the time, Pallas kernels for 0%

commit v1 on v0

v1 whole, which is shorter than its diff:
```python
import functools

import jax
import jax.numpy as jnp
from jax import lax
from jax.experimental import pallas as pl
from jax.experimental.pallas import tpu as pltpu
from jax.sharding import PartitionSpec as P

BLOCK = 64
ITERS = 2
LANES = 128
STEP = 8
WIDTH = 512
F32 = jnp.float32
BF16 = jnp.bfloat16
VMEM_BYTES = 56 * 1024 * 1024


def pad_rows(value, rows):
    missing = rows - value.shape[0]
    return jnp.concatenate([value, jnp.zeros((missing, value.shape[1]), value.dtype)], axis=0)


def spread_rows(source, target):
    for j in range(STEP):
        target[pl.ds(j * 8, 8), :] = jnp.broadcast_to(source[j : j + 1, :], (8, source.shape[1]))


def row_ids(rows, cols):
    return lax.broadcasted_iota(jnp.int32, (rows, cols), 0)


def forward_kernel(
    first, blocks, slabs_of, count, cam_ref, idx_ref, jc_ref, jp_ref, y_ref, proj_ref, *rest
):
    if first:
        table, yacc, spread, hacc = rest
    else:
        table, yacc, spread = rest
    step = pl.program_id(0)
    owners, _, rows, _ = cam_ref.shape
    slab_len = jc_ref.shape[2]
    parts, _, slabs, part_len = y_ref.shape

    @pl.when(step == 0)
    def _():
        table[...] = jnp.zeros_like(table)
        yacc[...] = jnp.zeros_like(yacc)
        if first:
            hacc[...] = jnp.zeros_like(hacc)
        for owner in range(owners):
            for k in range(9):
                value = cam_ref[owner, k]
                table[pl.ds(owner * rows * 24 + k, rows, stride=24), :] = value
                table[pl.ds(owner * rows * 24 + 9 + k, rows, stride=24), :] = value

    spread_rows(idx_ref, spread)
    row24 = row_ids(24, LANES)
    row8 = row_ids(8, LANES)

    def slot(j, carry):
        place = step * STEP + j
        block = blocks[place]
        slab = slabs_of[place]
        offset = (block % 2) * BLOCK
        here = table[pl.ds(pl.multiple_of((block // 2) * 24, 8), 24), :]
        for start in range(0, slab_len, LANES):
            cols = pl.ds(start, LANES)
            spot = pl.ds(pl.multiple_of((start // LANES * slabs + slab) * 8, 8), 8)
            index = spread[pl.ds(pl.multiple_of(j * 8, 8), 8), cols] + offset
            index = jnp.concatenate([index] * 3, axis=0)
            at_camera = jnp.take_along_axis(here, index, axis=1, mode="promise_in_bounds")
            prod = pad_rows(jc_ref[j, :, cols].astype(F32), 24) * at_camera
            zero = jnp.zeros_like(prod[:8])
            mid = prod[8:16]
            first_row = row8 < 1
            part0 = prod[0:8] + jnp.where(first_row, mid, zero)
            part1 = jnp.where(first_row, zero, mid) + prod[16:24]
            proj0 = jnp.sum(part0, axis=0, keepdims=True)
            proj1 = jnp.sum(part1, axis=0, keepdims=True)
            proj_ref[j, 0:1, cols] = proj0
            proj_ref[j, 1:2, cols] = proj1
            jp = pad_rows(jp_ref[j, :, cols].astype(F32), 8)
            pulled = jp * jnp.where(row8 < 3, proj0, proj1)
            yacc[spot, :] += pulled + pltpu.roll(pulled, 5, 0)
            if first:
                same = jp * jp
                near = jp * pltpu.roll(jp, 7, 0)
                far = jp * pltpu.roll(jp, 6, 0)
                same = same + pltpu.roll(same, 5, 0)
                near = near + pltpu.roll(near, 5, 0)
                far = far + pltpu.roll(far, 5, 0)
                packed = jnp.where(
                    row8 < 3,
                    same,
                    jnp.where(row8 < 5, pltpu.roll(near, 3, 0), pltpu.roll(far, 5, 0)),
                )
                hacc[spot, :] += packed
        return carry

    lax.fori_loop(0, jnp.clip(count[0] - step * STEP, 0, STEP), slot, 0)

    @pl.when(step == pl.num_programs(0) - 1)
    def _():
        for chunk in range(slab_len // LANES):
            part, cols = chunk * LANES // part_len, pl.ds(chunk * LANES % part_len, LANES)
            for group in range(slabs // 8):
                top = (chunk * slabs + group * 8) * 8
                down = pl.ds(group * 8, 8)
                for k in range(3):
                    y_ref[part, k, down, cols] = yacc[pl.ds(top + k, 8, stride=8), :]
                if first:
                    for k in range(6):
                        y_ref[part, 3 + k, down, cols] = hacc[pl.ds(top + k, 8, stride=8), :]


def backward_kernel(
    blocks, slabs_of, count, z_ref, proj_ref, idx_ref, jc_ref, jp_ref, out_ref, zrows, acc, spread
):
    step = pl.program_id(0)
    owners, _, rows, _ = out_ref.shape
    slab_len = jc_ref.shape[2]
    parts, _, slabs, part_len = z_ref.shape

    @pl.when(step == 0)
    def _():
        zrows[...] = jnp.zeros_like(zrows)
        acc[...] = jnp.zeros_like(acc)
        for chunk in range(slab_len // LANES):
            part, cols = chunk * LANES // part_len, pl.ds(chunk * LANES % part_len, LANES)
            for group in range(slabs // 8):
                top = (chunk * slabs + group * 8) * 8
                for k in range(3):
                    value = z_ref[part, k, pl.ds(group * 8, 8), cols]
                    zrows[pl.ds(top + k, 8, stride=8), :] = value
                    zrows[pl.ds(top + 3 + k, 8, stride=8), :] = value

    spread_rows(idx_ref, spread)
    row24 = row_ids(24, LANES)
    row8 = row_ids(8, LANES)
    cams = row_ids(BLOCK, LANES)
    half = lax.broadcasted_iota(jnp.int32, (16, LANES), 1) // BLOCK

    def slot(j, carry):
        place = step * STEP + j
        block = blocks[place]
        slab = slabs_of[place]
        total = jnp.zeros((48, BLOCK), F32)
        for outer in range(0, slab_len, WIDTH):
            values = []
            hots = []
            for start in range(outer, outer + WIDTH, LANES):
                cols = pl.ds(start, LANES)
                jp = pad_rows(jp_ref[j, :, cols].astype(F32), 8)
                spot = pl.ds(pl.multiple_of((start // LANES * slabs + slab) * 8, 8), 8)
                q = jp * zrows[spot, :]
                low3 = jnp.where(row8 < 3, q, jnp.zeros_like(q))
                miss0 = proj_ref[j, 0:1, cols] - jnp.sum(low3, axis=0, keepdims=True)
                miss1 = proj_ref[j, 1:2, cols] - jnp.sum(q - low3, axis=0, keepdims=True)
                pushed = pad_rows(jc_ref[j, :, cols].astype(F32), 24) * jnp.where(
                    row24 < 9, miss0, miss1
                )
                rest = pushed - pushed.astype(BF16).astype(F32)
                values.append(jnp.concatenate([pushed, rest], axis=0).astype(BF16))
                index = spread[pl.ds(pl.multiple_of(j * 8, 8), 8), cols]
                index = jnp.concatenate([index] * (BLOCK // 8), axis=0)
                hots.append(jnp.where(cams == index, 1.0, 0.0).astype(BF16))
            total = total + lax.dot_general(
                jnp.concatenate(values, axis=1),
                jnp.concatenate(hots, axis=1),
                (((1,), (1,)), ((), ())),
                preferred_element_type=F32,
            )
        both = total[0:24] + total[24:48]
        sums = both + pltpu.roll(both, 15, 0)
        wide = jnp.concatenate([sums[0:16], sums[0:16]], axis=1)
        where = pl.ds(pl.multiple_of((block // 2) * 16, 16), 16)
        acc[where, :] += jnp.where(half == block % 2, wide, jnp.zeros_like(wide))
        return carry

    lax.fori_loop(0, jnp.clip(count[0] - step * STEP, 0, STEP), slot, 0)

    @pl.when(step == pl.num_programs(0) - 1)
    def _():
        for owner in range(owners):
            for k in range(9):
                out_ref[owner, k] = acc[pl.ds(owner * rows * 16 + k, rows, stride=16), :]


def whole(shape):
    return pl.BlockSpec(shape, lambda i, *_: (0,) * len(shape))


def data_specs(pairs, slab_len):
    return [
        pl.BlockSpec((STEP, slab_len), lambda i, *_: (i, 0)),
        pl.BlockSpec((STEP, 18, slab_len), lambda i, *_: (i, 0, 0)),
        pl.BlockSpec((STEP, 6, slab_len), lambda i, *_: (i, 0, 0)),
    ]


def forward(first, lists, cams, idx, jc, jp, parts, slabs):
    pairs, slab_len = idx.shape
    owners, _, rows, _ = cams.shape
    part_len = slab_len // parts
    y_shape = (parts, 9 if first else 3, slabs, part_len)
    proj_spec = pl.BlockSpec((STEP, 2, slab_len), lambda i, *_: (i, 0, 0))
    out_shape = [
        jax.ShapeDtypeStruct(y_shape, F32),
        jax.ShapeDtypeStruct((pairs, 2, slab_len), F32),
    ]
    out_specs = [whole(y_shape), proj_spec]
    scratch = [
        pltpu.VMEM((owners * rows * 24, LANES), F32),
        pltpu.VMEM((slabs * 8 * (slab_len // LANES), LANES), F32),
        pltpu.VMEM((STEP * 8, slab_len), jnp.int32),
    ]
    if first:
        scratch.append(pltpu.VMEM((slabs * 8 * (slab_len // LANES), LANES), F32))
    return pl.pallas_call(
        functools.partial(forward_kernel, first),
        name="forward_first" if first else "forward_next",
        out_shape=out_shape,
        grid_spec=pltpu.PrefetchScalarGridSpec(
            num_scalar_prefetch=3,
            grid=(pairs // STEP,),
            in_specs=[whole(cams.shape)] + data_specs(pairs, slab_len),
            out_specs=out_specs,
            scratch_shapes=scratch,
        ),
        compiler_params=pltpu.CompilerParams(
            dimension_semantics=("arbitrary",), vmem_limit_bytes=VMEM_BYTES
        ),
    )(*lists, cams, idx, jc, jp)


def backward(lists, z, proj, idx, jc, jp, owners, rows):
    pairs, slab_len = idx.shape
    slabs = z.shape[2]
    out_shape = (owners, 9, rows, LANES)
    proj_spec = pl.BlockSpec((STEP, 2, slab_len), lambda i, *_: (i, 0, 0))
    return pl.pallas_call(
        backward_kernel,
        name="backward",
        out_shape=jax.ShapeDtypeStruct(out_shape, F32),
        grid_spec=pltpu.PrefetchScalarGridSpec(
            num_scalar_prefetch=3,
            grid=(pairs // STEP,),
            in_specs=[whole(z.shape), proj_spec] + data_specs(pairs, slab_len),
            out_specs=whole(out_shape),
            scratch_shapes=[
                pltpu.VMEM((slabs * 8 * (slab_len // LANES), LANES), F32),
                pltpu.VMEM((owners * rows * 16, LANES), F32),
                pltpu.VMEM((STEP * 8, slab_len), jnp.int32),
            ],
        ),
        compiler_params=pltpu.CompilerParams(
            dimension_semantics=("arbitrary",), vmem_limit_bytes=VMEM_BYTES
        ),
    )(*lists, z, proj, idx, jc, jp)


def swap_kernel(axis, gather, x_ref, out_ref, slots, send_sem, recv_sem):
    peers = lax.axis_size(axis)
    me = lax.axis_index(axis)
    barrier = pltpu.get_barrier_semaphore()
    for hop in range(1, peers):
        pl.semaphore_signal(
            barrier,
            inc=1,
            device_id={axis: lax.rem(me + hop, peers)},
            device_id_type=pl.DeviceIdType.MESH,
        )
    pl.semaphore_wait(barrier, peers - 1)
    copies = []
    for hop in range(1, peers):
        peer = lax.rem(me + hop, peers)
        copy = pltpu.make_async_remote_copy(
            src_ref=x_ref if gather else x_ref.at[peer],
            dst_ref=slots.at[hop - 1],
            send_sem=send_sem.at[hop - 1],
            recv_sem=recv_sem.at[hop - 1],
            device_id={axis: peer},
            device_id_type=pl.DeviceIdType.MESH,
        )
        copy.start()
        copies.append(copy)
    if gather:
        out_ref[me] = x_ref[...]
        for hop in range(1, peers):
            copies[hop - 1].wait()
            out_ref[lax.rem(me + peers - hop, peers)] = slots[hop - 1]
    else:
        for copy in copies:
            copy.wait()
        for k in range(out_ref.shape[0]):
            total = x_ref[me, k]
            for hop in range(1, peers):
                total = total + slots[hop - 1, k]
            out_ref[k] = total


def swap(value, axis, gather, ident):
    peers = lax.axis_size(axis)
    piece = value.shape if gather else value.shape[1:]
    out = (peers,) + piece if gather else piece
    return pl.pallas_call(
        functools.partial(swap_kernel, axis, gather),
        name=("gather_" if gather else "scatter_") + axis,
        out_shape=jax.ShapeDtypeStruct(out, F32),
        in_specs=[pl.BlockSpec(memory_space=pltpu.VMEM)],
        out_specs=pl.BlockSpec(memory_space=pltpu.VMEM),
        scratch_shapes=[
            pltpu.VMEM((peers - 1,) + piece, F32),
            pltpu.SemaphoreType.DMA((peers - 1,)),
            pltpu.SemaphoreType.DMA((peers - 1,)),
        ],
        compiler_params=pltpu.CompilerParams(
            collective_id=ident, has_side_effects=True, vmem_limit_bytes=24 * 1024 * 1024
        ),
    )(value)


def tile_of(values):
    return jnp.broadcast_to(jnp.stack(values)[:, None, None], (len(values), 8, LANES))


def over_cam(values):
    padded = values + [jnp.zeros((), F32)] * (2 - len(values))
    return jnp.sum(swap(tile_of(padded), "cam", True, 6)[:, :, 0, 0], axis=0)


def over_pt(value):
    return jnp.sum(swap(tile_of([value]), "pt", True, 5)[:, 0, 0, 0])


def invert_points(hess, damping):
    entry_xx = hess[0] + damping
    entry_yy = hess[1] + damping
    entry_zz = hess[2] + damping
    entry_xy = hess[3]
    entry_yz = hess[4]
    entry_xz = hess[5]
    cof_xx = entry_yy * entry_zz - entry_yz * entry_yz
    cof_xy = entry_xz * entry_yz - entry_xy * entry_zz
    cof_xz = entry_xy * entry_yz - entry_xz * entry_yy
    cof_yy = entry_xx * entry_zz - entry_xz * entry_xz
    cof_yz = entry_xy * entry_xz - entry_xx * entry_yz
    cof_zz = entry_xx * entry_yy - entry_xy * entry_xy
    determinant = entry_xx * cof_xx + entry_xy * cof_xy + entry_xz * cof_xz
    return [
        cof / determinant for cof in (cof_xx, cof_xy, cof_xz, cof_yy, cof_yz, cof_zz)
    ]


def apply_inverse(inverse, vector):
    out_x = inverse[0] * vector[0] + inverse[1] * vector[1] + inverse[2] * vector[2]
    out_y = inverse[1] * vector[0] + inverse[3] * vector[1] + inverse[4] * vector[2]
    out_z = inverse[2] * vector[0] + inverse[4] * vector[1] + inverse[5] * vector[2]
    return jnp.stack([out_x, out_y, out_z])


def per_device(
    right_side,
    cam_damping,
    point_damping,
    block_ids,
    slab_ids,
    cam_index,
    cam_jacobian,
    point_jacobian,
    pair_count,
):
    pairs = block_ids.shape[2]
    slab_len = cam_index.shape[3]
    slabs = point_damping.shape[0] // slab_len
    cam_dev = right_side.shape[1]
    rows = cam_dev // LANES
    owners = lax.axis_size("pt")
    parts = lax.axis_size("cam")
    part_len = slab_len // parts
    lists = (block_ids.reshape(pairs), slab_ids.reshape(pairs), pair_count.reshape(1))
    idx = cam_index.reshape(pairs, slab_len)
    jc = cam_jacobian.reshape(pairs, 18, slab_len)
    jp = point_jacobian.reshape(pairs, 6, slab_len)
    residual = right_side.reshape(9, rows, LANES)
    damping = cam_damping.reshape(9, rows, LANES)
    part = lax.axis_index("cam")
    point_damp = lax.dynamic_slice_in_dim(
        point_damping.reshape(slabs, slab_len), part * part_len, part_len, 1
    )
    direction = residual
    answer = jnp.zeros_like(residual)
    cams = swap(direction, "pt", True, 0)
    norm_group = jnp.sum(cams * cams)
    norm_now = None
    inverse = None
    for iteration in range(ITERS):
        if iteration == 0:
            y, proj = forward(True, lists, cams, idx, jc, jp, parts, slabs)
            merged = swap(y, "cam", False, 1)
            pulled = merged[:3]
            inverse = invert_points(merged[3:], point_damp)
        else:
            y, proj = forward(False, lists, cams, idx, jc, jp, parts, slabs)
            pulled = swap(y, "cam", False, 2)
        z = swap(apply_inverse(inverse, pulled), "cam", True, 3)
        sums = backward(lists, z, proj, idx, jc, jp, owners, rows)
        image = damping * direction + swap(sums, "pt", False, 4)
        curve = over_pt(jnp.sum(direction * image))
        if iteration == 0:
            both = over_cam([curve, norm_group])
            curve, norm_now = both[0], both[1]
        else:
            curve = over_cam([curve])[0]
        step_size = norm_now / curve
        answer = answer + step_size * direction
        residual = residual - step_size * image
        if iteration + 1 < ITERS:
            group = swap(residual, "pt", True, 0)
            norm_next = over_cam([jnp.sum(group * group)])[0]
            ratio = norm_next / norm_now
            cams = group + ratio * cams
            direction = residual + ratio * direction
            norm_now = norm_next
    return answer.reshape(9, cam_dev), residual.reshape(9, cam_dev)


def solution(mesh):
    in_specs = (
        P(None, ("cam", "pt")),
        P(None, ("cam", "pt")),
        P("pt"),
        P("cam", "pt", None),
        P("cam", "pt", None),
        P("cam", "pt", None, None),
        P("cam", "pt", None, None, None),
        P("cam", "pt", None, None, None),
        P("cam", "pt"),
    )
    out_specs = (P(None, ("cam", "pt")), P(None, ("cam", "pt")))
    return jax.shard_map(
        per_device, mesh=mesh, in_specs=in_specs, out_specs=out_specs, check_vma=False
    )
```

time: 747 us -> 308 us (0.41); the launches traced: 737 us -> 313 us
  Pallas kernels: 0 us -> 273 us
  waiting for transfers between devices: 233 us -> 0 us
  matrix products: 159 us -> 0 us
  local copies, waits for them, and re-layouts: 153 us -> 28.9 us
  blocking collectives: 92.2 us -> 0 us
  other arithmetic: 79.7 us -> 8.33 us
  between operations: 19.2 us -> 3.55 us
    pallas_call x0 -> x17, Pallas kernels: none -> 273 us  [the longest x13 206 us: swap(): pl.pallas_call(functools.partial(swap_kernel, axis, gather), name=('gathe...]
    psum x4 -> x0, waiting for transfers between devices: 233 us -> none  [the longest x2 128 us: per_device(): lax.psum(group_sum.reshape(9, blk_group * BLOCK), 'pt')]
    dot_general x39 -> x0, matrix products: 159 us -> none  [the longest x16 74.6 us: camera_per_group(): return jnp.einsum('gkn,gnb->gkb', pushed_group, one_hot, precision=HIGH)]
    all_gather x2 -> x0, blocking collectives: 71.4 us -> none  [the longest x1 36.7 us: per_device(): lax.all_gather(cam_damping, 'pt', axis=1, tiled=True)]
    reduce_sum x12 -> x9, other arithmetic: 53 us -> 4.34 us  [the longest x2 1.25 us: per_device(): curve = over_pt(jnp.sum(direction * image))]
    another operation x12 -> x0, local copies, waits for them, and re-layouts: 31.4 us -> none
    mul x2 -> x0, local copies, waits for them, and re-layouts: 29.7 us -> none  [project(): return jnp.sum(cam_jac * at_camera[:, None], axis=2)]
    eq x32 -> x0, local copies, waits for them, and re-layouts: 29.3 us -> none  [the longest x16 14.7 us: camera_per_group(): index_group[:, :, None] == jnp.arange(BLOCK, dtype=jnp.int32)[None, None, :]]
  transfers between devices with their start and end apart: 4 -> 0, of which waited for: 4 -> 0; matrix products, arithmetic and copies ran while one was open for 0% -> 0% of each run, Pallas kernels for 0% -> 0%
where the time goes in v1:
time: 308 us; the launch traced here: 313 us
  Pallas kernels  273 us (89%)
  local copies, waits for them, and re-layouts  28.9 us (9%)
  other arithmetic  8.33 us (3%)
  between operations  3.55 us (1%)
    pallas_call x13, Pallas kernels, swap(): pl.pallas_call(functools.partial(swap_kernel, axis, gather), name=('gathe...  206 us
    pallas_call x2, Pallas kernels, backward(): pl.pallas_call(backward_kernel, name='backward', out_shape=jax.ShapeDtype...  35.3 us
    pallas_call x2, Pallas kernels, forward(): pl.pallas_call(functools.partial(forward_kernel, first), name='forward_fi...  31.5 us
    unnamed x30, local copies, waits for them, and re-layouts  26.7 us

profile of v1, /device:TPU:0, one launch (start us, length us, event | category | flops | bytes accessed | tf_op | source)
XLA Modules:
  0.0 313.2 jit_solution(2424793337685621400)
XLA Ops:
  1.6 15.7 %gather_pt.4.cam_ref = f32[8,9,16,128]{3,2,1,0:T(8,128)S(1)} custom-call(f32[9,16,128]{2,1,0:T(8,128)S(1)} %slice.107.x_ref), custom_call_target="tpu_custom_call" | custom-call | tf_op jit(solution)/shard_map/gather_pt/pallas_call | solution.py:308
  17.3 13.9 %copy.19 = bf16[1,1,64,18,4096]{4,3,2,1,0:T(8,128)(2,1)} copy(bf16[1,1,64,18,4096]{4,2,3,1,0:T(8,128)(2,1)} %param.15) | data formatting | bytes 18874368 | tf_op args[6]
  31.2 3.7 %copy.20 = bf16[1,1,64,6,4096]{4,3,2,1,0:T(8,128)(2,1)} copy(bf16[1,1,64,6,4096]{4,2,3,1,0:T(8,128)(2,1)S(1)} %copy-done.8) | data formatting | bytes 6291456 | tf_op args[7]
  35.6 16.3 %forward_first.1 = (f32[4,9,16,1024]{3,2,1,0:T(8,128)}, f32[64,2,4096]{2,1,0:T(2,128)}) custom-call(s32[64]{0:T(128)} %bitcast.227, s32[64]{0:T(128)} %bitcast.231, s32[1]{0:T(128)} %bitcast.196.count, f32[8,9,16,128]{3,2,1,0:T(8,128)} %copy-done, s32[64,4096]{1,0:T(8,128)} %bitcast.208, bf16[64,18,4096]{2,1,0:T(8,128)(2,1)} %bitcast.200, ...), custom_call_target="tpu_custom_call" | custom-call | tf_op jit(solution)/shard_map/forward_first/pallas_call | solution.py:221
  51.8 1.7 copy-done.6
  53.5 29.7 %scatter_cam.2 = f32[9,16,1024]{2,1,0:T(8,128)S(1)} custom-call(f32[4,9,16,1024]{3,2,1,0:T(8,128)S(1)} %copy-done.6), custom_call_target="tpu_custom_call" | custom-call | tf_op jit(solution)/shard_map/scatter_cam/pallas_call | solution.py:308
  83.5 11.0 %gather_cam.5.z_ref = f32[4,3,16,1024]{3,2,1,0:T(8,128)S(1)} custom-call(f32[3,16,1024]{2,1,0:T(8,128)S(1)} %pad_maximum_fusion.x_ref), custom_call_target="tpu_custom_call" | custom-call | tf_op jit(solution)/shard_map/gather_cam/pallas_call | solution.py:308
  95.3 17.7 %backward.2.x_ref = f32[8,9,16,128]{3,2,1,0:T(8,128)} custom-call(s32[64]{0:T(128)} %bitcast.228, s32[64]{0:T(128)} %bitcast.232, s32[1]{0:T(128)} %bitcast.197.count, f32[4,3,16,1024]{3,2,1,0:T(8,128)} %copy-done.3, f32[64,2,4096]{2,1,0:T(2,128)} %get-tuple-element.7.proj_ref, s32[64,4096]{1,0:T(8,128)} %bitcast.209, bf16[64,18,4096]{2,1,0:T(8,128)(2,1)} %bitcast.201, ...), custom_call_target="tpu_custom_call" | custom-call | tf_op jit(solution)/shard_map/backward/pallas_call | solution.py:243
  113.1 1.1 copy-done.5
  114.1 36.4 %scatter_pt.2 = f32[9,16,128]{2,1,0:T(8,128)S(1)} custom-call(f32[8,9,16,128]{3,2,1,0:T(8,128)S(1)} %copy-done.5), custom_call_target="tpu_custom_call" | custom-call | tf_op jit(solution)/shard_map/scatter_pt/pallas_call | solution.py:308
  151.8 12.4 %gather_pt.5 = f32[8,1,8,128]{3,2,1,0:T(8,128)S(1)} custom-call(f32[1,8,128]{2,1,0:T(8,128)S(1)} %broadcast_in_dim.10.x_ref), custom_call_target="tpu_custom_call" | custom-call | tf_op jit(solution)/shard_map/gather_pt/pallas_call | solution.py:308
  165.6 1.3 pad_maximum_fusion.4
  166.9 5.1 %gather_cam.6 = f32[4,2,8,128]{3,2,1,0:T(8,128)S(1)} custom-call(f32[2,8,128]{2,1,0:T(8,128)S(1)} %broadcast_in_dim.11.x_ref), custom_call_target="tpu_custom_call" | custom-call | tf_op jit(solution)/shard_map/gather_cam/pallas_call | solution.py:308
  174.0 13.8 %gather_pt.6 = f32[8,9,16,128]{3,2,1,0:T(8,128)S(1)} custom-call(f32[9,16,128]{2,1,0:T(8,128)S(1)} %multiply_subtract_fusion.1.x_ref), custom_call_target="tpu_custom_call" | custom-call | tf_op jit(solution)/shard_map/gather_pt/pallas_call | solution.py:308
  189.5 3.7 %gather_cam.7 = f32[4,2,8,128]{3,2,1,0:T(8,128)S(1)} custom-call(f32[2,8,128]{2,1,0:T(8,128)S(1)} %broadcast_in_dim.12.x_ref), custom_call_target="tpu_custom_call" | custom-call | tf_op jit(solution)/shard_map/gather_cam/pallas_call | solution.py:308
  194.8 15.2 %forward_next.1 = (f32[4,3,16,1024]{3,2,1,0:T(8,128)}, f32[64,2,4096]{2,1,0:T(2,128)}) custom-call(s32[64]{0:T(128)} %bitcast.229, s32[64]{0:T(128)} %bitcast.233, s32[1]{0:T(128)} %bitcast.198.count, f32[8,9,16,128]{3,2,1,0:T(8,128)} %multiply_add_fusion.cam_ref, s32[64,4096]{1,0:T(8,128)} %bitcast.210, bf16[64,18,4096]{2,1,0:T(8,128)(2,1)} %bitcast.202, ...), custom_call_target="tpu_custom_call" | custom-call | tf_op jit(solution)/shard_map/forward_next/pallas_call | solution.py:221
  210.0 1.1 copy-done.7
  211.2 13.9 %scatter_cam.3 = f32[3,16,1024]{2,1,0:T(8,128)S(1)} custom-call(f32[4,3,16,1024]{3,2,1,0:T(8,128)S(1)} %copy-done.7), custom_call_target="tpu_custom_call" | custom-call | tf_op jit(solution)/shard_map/scatter_cam/pallas_call | solution.py:308
  225.1 11.0 %gather_cam.8.z_ref = f32[4,3,16,1024]{3,2,1,0:T(8,128)S(1)} custom-call(f32[3,16,1024]{2,1,0:T(8,128)S(1)} %pad_maximum_fusion.1.x_ref), custom_call_target="tpu_custom_call" | custom-call | tf_op jit(solution)/shard_map/gather_cam/pallas_call | solution.py:308
  237.0 17.6 %backward.3.x_ref = f32[8,9,16,128]{3,2,1,0:T(8,128)} custom-call(s32[64]{0:T(128)} %bitcast.230, s32[64]{0:T(128)} %bitcast.234, s32[1]{0:T(128)} %bitcast.199.count, f32[4,3,16,1024]{3,2,1,0:T(8,128)} %copy-done.2, f32[64,2,4096]{2,1,0:T(2,128)} %get-tuple-element.9.proj_ref, s32[64,4096]{1,0:T(8,128)} %bitcast.211, bf16[64,18,4096]{2,1,0:T(8,128)(2,1)} %bitcast.203, ...), custom_call_target="tpu_custom_call" | custom-call | tf_op jit(solution)/shard_map/backward/pallas_call | solution.py:243
  254.6 1.1 copy-done.4
  255.7 36.9 %scatter_pt.3 = f32[9,16,128]{2,1,0:T(8,128)S(1)} custom-call(f32[8,9,16,128]{3,2,1,0:T(8,128)S(1)} %copy-done.4), custom_call_target="tpu_custom_call" | custom-call | tf_op jit(solution)/shard_map/scatter_pt/pallas_call | solution.py:308
  293.9 11.9 %gather_pt.7 = f32[8,1,8,128]{3,2,1,0:T(8,128)S(1)} custom-call(f32[1,8,128]{2,1,0:T(8,128)S(1)} %broadcast_in_dim.13.x_ref), custom_call_target="tpu_custom_call" | custom-call | tf_op jit(solution)/shard_map/gather_pt/pallas_call | solution.py:308
  307.2 4.4 %gather_cam.9 = f32[4,2,8,128]{3,2,1,0:T(8,128)S(1)} custom-call(f32[2,8,128]{2,1,0:T(8,128)S(1)} %broadcast_in_dim.14.x_ref), custom_call_target="tpu_custom_call" | custom-call | tf_op jit(solution)/shard_map/gather_cam/pallas_call | solution.py:308
  (53 shorter events, 13.4 us)
Async XLA Ops:
  17.3 13.9 %copy-start = (f32[8,9,16,128]{3,2,1,0:T(8,128)}, f32[8,9,16,128]{3,2,1,0:T(8,128)S(1)}, u32[]{:S(2)}) copy-start(f32[8,9,16,128]{3,2,1,0:T(8,128)S(1)} %gather_pt.4.cam_ref) | copy-start | bytes 1769476
  17.3 13.9 %copy-start.8 = (bf16[1,1,64,6,4096]{4,2,3,1,0:T(8,128)(2,1)S(1)}, bf16[1,1,64,6,4096]{4,2,3,1,0:T(8,128)(2,1)}, u32[]{:S(2)}) copy-start(bf16[1,1,64,6,4096]{4,2,3,1,0:T(8,128)(2,1)} %param.16) | copy-start | bytes 9437188
  35.5 47.6 %copy-start.9 = (f32[65536]{0:T(1024)S(1)}, f32[65536]{0:T(1024)}, u32[]{:S(2)}) copy-start(f32[65536]{0:T(1024)} %param.11) | copy-start | bytes 786436
  51.8 1.7 copy-start.6
  94.4 0.9 copy-start.3
  95.3 55.2 %copy-start.10 = (f32[9,2048]{1,0:T(8,128)S(1)}, f32[9,2048]{1,0:T(8,128)}, u32[]{:S(2)}) copy-start(f32[9,2048]{1,0:T(8,128)} %param.10) | copy-start | bytes 221188
  95.3 69.5 %copy-start.1 = (f32[8,9,16,128]{3,2,1,0:T(8,128)S(1)}, f32[8,9,16,128]{3,2,1,0:T(8,128)}, u32[]{:S(2)}) copy-start(f32[8,9,16,128]{3,2,1,0:T(8,128)} %copy-done) | copy-start | bytes 1769476
  113.1 1.1 copy-start.5
  210.0 1.1 copy-start.7
  236.1 0.9 copy-start.2
  254.6 1.1 copy-start.4

commit v2 on v1

--- a/solution.py
+++ b/solution.py
@@ -34,69 +34,55 @@
 def forward_kernel(
     first, blocks, slabs_of, count, cam_ref, idx_ref, jc_ref, jp_ref, y_ref, proj_ref, *rest
 ):
-    if first:
-        table, yacc, spread, hacc = rest
-    else:
-        table, yacc, spread = rest
+    table, yacc, stage, tables, shift = rest
     step = pl.program_id(0)
     owners, _, rows, _ = cam_ref.shape
     slab_len = jc_ref.shape[2]
-    parts, _, slabs, part_len = y_ref.shape
+    parts, fields, slabs, part_len = y_ref.shape
+    tall = 16 if first else 8
 
     @pl.when(step == 0)
     def _():
         table[...] = jnp.zeros_like(table)
         yacc[...] = jnp.zeros_like(yacc)
-        if first:
-            hacc[...] = jnp.zeros_like(hacc)
+        stage[...] = jnp.zeros_like(stage)
         for owner in range(owners):
             for k in range(9):
-                value = cam_ref[owner, k]
-                table[pl.ds(owner * rows * 24 + k, rows, stride=24), :] = value
-                table[pl.ds(owner * rows * 24 + 9 + k, rows, stride=24), :] = value
-
-    spread_rows(idx_ref, spread)
-    row24 = row_ids(24, LANES)
-    row8 = row_ids(8, LANES)
+                table[pl.ds(owner * rows * 16 + k, rows, stride=16), :] = cam_ref[owner, k]
+
+    @pl.when(step * STEP < count[0])
+    def _():
+        for j in range(STEP):
+            block = blocks[step * STEP + j]
+            here = table[pl.ds(pl.multiple_of((block // 2) * 16, 16), 16), :]
+            tables[pl.ds(j, 16, stride=8), :] = here
+            shift[j : j + 1, :] = jnp.full((1, LANES), (block % 2) * BLOCK, jnp.int32)
+        for chunk in range(slab_len // LANES):
+            cols = pl.ds(chunk * LANES, LANES)
+            index = idx_ref[:, cols] + shift[...]
+            proj = [None, None]
+            for k in range(9):
+                at_camera = jnp.take_along_axis(
+                    tables[pl.ds(k * 8, 8), :], index, axis=1, mode="promise_in_bounds"
+                )
+                for i in range(2):
+                    term = jc_ref[9 * i + k, :, cols].astype(F32) * at_camera
+                    proj[i] = term if k == 0 else proj[i] + term
+            jp = [jp_ref[k, :, cols].astype(F32) for k in range(6)]
+            made = [jp[k] * proj[0] + jp[3 + k] * proj[1] for k in range(3)]
+            if first:
+                pairs = [(0, 0), (1, 1), (2, 2), (0, 1), (1, 2), (0, 2)]
+                made += [jp[a] * jp[b] + jp[3 + a] * jp[3 + b] for a, b in pairs]
+            for i in range(2):
+                proj_ref[i, :, cols] = proj[i]
+            for k, value in enumerate(made):
+                stage[pl.ds(chunk * 128 + k, 8, stride=16), :] = value
 
     def slot(j, carry):
-        place = step * STEP + j
-        block = blocks[place]
-        slab = slabs_of[place]
-        offset = (block % 2) * BLOCK
-        here = table[pl.ds(pl.multiple_of((block // 2) * 24, 8), 24), :]
-        for start in range(0, slab_len, LANES):
-            cols = pl.ds(start, LANES)
-            spot = pl.ds(pl.multiple_of((start // LANES * slabs + slab) * 8, 8), 8)
-            index = spread[pl.ds(pl.multiple_of(j * 8, 8), 8), cols] + offset
-            index = jnp.concatenate([index] * 3, axis=0)
-            at_camera = jnp.take_along_axis(here, index, axis=1, mode="promise_in_bounds")
-            prod = pad_rows(jc_ref[j, :, cols].astype(F32), 24) * at_camera
-            zero = jnp.zeros_like(prod[:8])
-            mid = prod[8:16]
-            first_row = row8 < 1
-            part0 = prod[0:8] + jnp.where(first_row, mid, zero)
-            part1 = jnp.where(first_row, zero, mid) + prod[16:24]
-            proj0 = jnp.sum(part0, axis=0, keepdims=True)
-            proj1 = jnp.sum(part1, axis=0, keepdims=True)
-            proj_ref[j, 0:1, cols] = proj0
-            proj_ref[j, 1:2, cols] = proj1
-            jp = pad_rows(jp_ref[j, :, cols].astype(F32), 8)
-            pulled = jp * jnp.where(row8 < 3, proj0, proj1)
-            yacc[spot, :] += pulled + pltpu.roll(pulled, 5, 0)
-            if first:
-                same = jp * jp
-                near = jp * pltpu.roll(jp, 7, 0)
-                far = jp * pltpu.roll(jp, 6, 0)
-                same = same + pltpu.roll(same, 5, 0)
-                near = near + pltpu.roll(near, 5, 0)
-                far = far + pltpu.roll(far, 5, 0)
-                packed = jnp.where(
-                    row8 < 3,
-                    same,
-                    jnp.where(row8 < 5, pltpu.roll(near, 3, 0), pltpu.roll(far, 5, 0)),
-                )
-                hacc[spot, :] += packed
+        slab = slabs_of[step * STEP + j]
+        for chunk in range(slab_len // LANES):
+            spot = pl.ds(pl.multiple_of((chunk * slabs + slab) * tall, 8), tall)
+            yacc[spot, :] += stage[pl.ds(pl.multiple_of(chunk * 128 + j * 16, 16), tall), :]
         return carry
 
     lax.fori_loop(0, jnp.clip(count[0] - step * STEP, 0, STEP), slot, 0)
@@ -106,17 +92,16 @@
         for chunk in range(slab_len // LANES):
             part, cols = chunk * LANES // part_len, pl.ds(chunk * LANES % part_len, LANES)
             for group in range(slabs // 8):
-                top = (chunk * slabs + group * 8) * 8
-                down = pl.ds(group * 8, 8)
-                for k in range(3):
-                    y_ref[part, k, down, cols] = yacc[pl.ds(top + k, 8, stride=8), :]
-                if first:
-                    for k in range(6):
-                        y_ref[part, 3 + k, down, cols] = hacc[pl.ds(top + k, 8, stride=8), :]
+                top = (chunk * slabs + group * 8) * tall
+                for k in range(fields):
+                    y_ref[part, k, pl.ds(group * 8, 8), cols] = yacc[
+                        pl.ds(top + k, 8, stride=tall), :
+                    ]
 
 
 def backward_kernel(
-    blocks, slabs_of, count, z_ref, proj_ref, idx_ref, jc_ref, jp_ref, out_ref, zrows, acc, spread
+    blocks, slabs_of, count, z_ref, proj_ref, idx_ref, jc_ref, jp_ref, out_ref,
+    zrows, acc, spread, stage, zslot,
 ):
     step = pl.program_id(0)
     owners, _, rows, _ = out_ref.shape
@@ -127,40 +112,49 @@
     def _():
         zrows[...] = jnp.zeros_like(zrows)
         acc[...] = jnp.zeros_like(acc)
+        stage[...] = jnp.zeros_like(stage)
         for chunk in range(slab_len // LANES):
             part, cols = chunk * LANES // part_len, pl.ds(chunk * LANES % part_len, LANES)
             for group in range(slabs // 8):
                 top = (chunk * slabs + group * 8) * 8
                 for k in range(3):
-                    value = z_ref[part, k, pl.ds(group * 8, 8), cols]
-                    zrows[pl.ds(top + k, 8, stride=8), :] = value
-                    zrows[pl.ds(top + 3 + k, 8, stride=8), :] = value
-
-    spread_rows(idx_ref, spread)
-    row24 = row_ids(24, LANES)
-    row8 = row_ids(8, LANES)
+                    zrows[pl.ds(top + k, 8, stride=8), :] = z_ref[
+                        part, k, pl.ds(group * 8, 8), cols
+                    ]
+
+    @pl.when(step * STEP < count[0])
+    def _():
+        spread_rows(idx_ref, spread)
+        for j in range(STEP):
+            slab = slabs_of[step * STEP + j]
+            for chunk in range(slab_len // LANES):
+                spot = pl.ds(pl.multiple_of((chunk * slabs + slab) * 8, 8), 8)
+                zslot[pl.ds(chunk * 64 + j, 8, stride=8), :] = zrows[spot, :]
+        for chunk in range(slab_len // LANES):
+            cols = pl.ds(chunk * LANES, LANES)
+            miss = [proj_ref[i, :, cols] for i in range(2)]
+            for k in range(3):
+                z = zslot[pl.ds(chunk * 64 + k * 8, 8), :]
+                for i in range(2):
+                    miss[i] = miss[i] - jp_ref[3 * i + k, :, cols].astype(F32) * z
+            for k in range(9):
+                stage[pl.ds(chunk * 128 + k, 8, stride=16), :] = (
+                    jc_ref[k, :, cols].astype(F32) * miss[0]
+                    + jc_ref[9 + k, :, cols].astype(F32) * miss[1]
+                )
+
     cams = row_ids(BLOCK, LANES)
     half = lax.broadcasted_iota(jnp.int32, (16, LANES), 1) // BLOCK
 
     def slot(j, carry):
-        place = step * STEP + j
-        block = blocks[place]
-        slab = slabs_of[place]
-        total = jnp.zeros((48, BLOCK), F32)
+        block = blocks[step * STEP + j]
+        total = jnp.zeros((32, BLOCK), F32)
         for outer in range(0, slab_len, WIDTH):
             values = []
             hots = []
             for start in range(outer, outer + WIDTH, LANES):
                 cols = pl.ds(start, LANES)
-                jp = pad_rows(jp_ref[j, :, cols].astype(F32), 8)
-                spot = pl.ds(pl.multiple_of((start // LANES * slabs + slab) * 8, 8), 8)
-                q = jp * zrows[spot, :]
-                low3 = jnp.where(row8 < 3, q, jnp.zeros_like(q))
-                miss0 = proj_ref[j, 0:1, cols] - jnp.sum(low3, axis=0, keepdims=True)
-                miss1 = proj_ref[j, 1:2, cols] - jnp.sum(q - low3, axis=0, keepdims=True)
-                pushed = pad_rows(jc_ref[j, :, cols].astype(F32), 24) * jnp.where(
-                    row24 < 9, miss0, miss1
-                )
+                pushed = stage[pl.ds(pl.multiple_of(start + j * 16, 16), 16), :]
                 rest = pushed - pushed.astype(BF16).astype(F32)
                 values.append(jnp.concatenate([pushed, rest], axis=0).astype(BF16))
                 index = spread[pl.ds(pl.multiple_of(j * 8, 8), 8), cols]
@@ -172,9 +166,8 @@
                 (((1,), (1,)), ((), ())),
                 preferred_element_type=F32,
             )
-        both = total[0:24] + total[24:48]
-        sums = both + pltpu.roll(both, 15, 0)
-        wide = jnp.concatenate([sums[0:16], sums[0:16]], axis=1)
+        sums = total[0:16] + total[16:32]
+        wide = jnp.concatenate([sums, sums], axis=1)
         where = pl.ds(pl.multiple_of((block // 2) * 16, 16), 16)
         acc[where, :] += jnp.where(half == block % 2, wide, jnp.zeros_like(wide))
         return carry
@@ -195,8 +188,8 @@
 def data_specs(pairs, slab_len):
     return [
         pl.BlockSpec((STEP, slab_len), lambda i, *_: (i, 0)),
-        pl.BlockSpec((STEP, 18, slab_len), lambda i, *_: (i, 0, 0)),
-        pl.BlockSpec((STEP, 6, slab_len), lambda i, *_: (i, 0, 0)),
+        pl.BlockSpec((18, STEP, slab_len), lambda i, *_: (0, i, 0)),
+        pl.BlockSpec((6, STEP, slab_len), lambda i, *_: (0, i, 0)),
     ]
 
 
@@ -205,19 +198,19 @@
     owners, _, rows, _ = cams.shape
     part_len = slab_len // parts
     y_shape = (parts, 9 if first else 3, slabs, part_len)
-    proj_spec = pl.BlockSpec((STEP, 2, slab_len), lambda i, *_: (i, 0, 0))
+    proj_spec = pl.BlockSpec((2, STEP, slab_len), lambda i, *_: (0, i, 0))
     out_shape = [
         jax.ShapeDtypeStruct(y_shape, F32),
-        jax.ShapeDtypeStruct((pairs, 2, slab_len), F32),
+        jax.ShapeDtypeStruct((2, pairs, slab_len), F32),
     ]
     out_specs = [whole(y_shape), proj_spec]
     scratch = [
-        pltpu.VMEM((owners * rows * 24, LANES), F32),
-        pltpu.VMEM((slabs * 8 * (slab_len // LANES), LANES), F32),
-        pltpu.VMEM((STEP * 8, slab_len), jnp.int32),
+        pltpu.VMEM((owners * rows * 16, LANES), F32),
+        pltpu.VMEM((slabs * (16 if first else 8) * (slab_len // LANES), LANES), F32),
+        pltpu.VMEM((slab_len, LANES), F32),
+        pltpu.VMEM((16 * STEP, LANES), F32),
+        pltpu.VMEM((STEP, LANES), jnp.int32),
     ]
-    if first:
-        scratch.append(pltpu.VMEM((slabs * 8 * (slab_len // LANES), LANES), F32))
     return pl.pallas_call(
         functools.partial(forward_kernel, first),
         name="forward_first" if first else "forward_next",
@@ -239,7 +232,7 @@
     pairs, slab_len = idx.shape
     slabs = z.shape[2]
     out_shape = (owners, 9, rows, LANES)
-    proj_spec = pl.BlockSpec((STEP, 2, slab_len), lambda i, *_: (i, 0, 0))
+    proj_spec = pl.BlockSpec((2, STEP, slab_len), lambda i, *_: (0, i, 0))
     return pl.pallas_call(
         backward_kernel,
         name="backward",
@@ -253,6 +246,8 @@
                 pltpu.VMEM((slabs * 8 * (slab_len // LANES), LANES), F32),
                 pltpu.VMEM((owners * rows * 16, LANES), F32),
                 pltpu.VMEM((STEP * 8, slab_len), jnp.int32),
+                pltpu.VMEM((slab_len, LANES), F32),
+                pltpu.VMEM((slab_len // 2, LANES), F32),
             ],
         ),
         compiler_params=pltpu.CompilerParams(
@@ -382,8 +377,8 @@
     part_len = slab_len // parts
     lists = (block_ids.reshape(pairs), slab_ids.reshape(pairs), pair_count.reshape(1))
     idx = cam_index.reshape(pairs, slab_len)
-    jc = cam_jacobian.reshape(pairs, 18, slab_len)
-    jp = point_jacobian.reshape(pairs, 6, slab_len)
+    jc = cam_jacobian.reshape(pairs, 18, slab_len).transpose(1, 0, 2)
+    jp = point_jacobian.reshape(pairs, 6, slab_len).transpose(1, 0, 2)
     residual = right_side.reshape(9, rows, LANES)
     damping = cam_damping.reshape(9, rows, LANES)
     part = lax.axis_index("cam")

time: 308 us -> 267 us (0.87); the launches traced: 313 us -> 266 us
  Pallas kernels: 273 us -> 242 us
  local copies, waits for them, and re-layouts: 28.9 us -> 12.1 us
    pallas_call x13, Pallas kernels: 206 us -> 184 us  [swap(): pl.pallas_call(functools.partial(swap_kernel, axis, gather), name=('gathe...]
    unnamed x30 -> x26, local copies, waits for them, and re-layouts: 26.7 us -> 9.89 us
    pallas_call x2, Pallas kernels: 31.5 us -> 24.4 us  [forward(): pl.pallas_call(functools.partial(forward_kernel, first), name='forward_fi...]
where the time goes in v2:
time: 267 us; the launch traced here: 266 us
  Pallas kernels  242 us (91%)
  local copies, waits for them, and re-layouts  12.1 us (5%)
  other arithmetic  8.33 us (3%)
  between operations  3.79 us (1%)
    pallas_call x13, Pallas kernels, swap(): pl.pallas_call(functools.partial(swap_kernel, axis, gather), name=('gathe...  184 us
    pallas_call x2, Pallas kernels, backward(): pl.pallas_call(backward_kernel, name='backward', out_shape=jax.ShapeDtype...  33.9 us
    pallas_call x2, Pallas kernels, forward(): pl.pallas_call(functools.partial(forward_kernel, first), name='forward_fi...  24.4 us
    unnamed x26, local copies, waits for them, and re-layouts  9.89 us

profile of v2, /device:TPU:0, one launch (start us, length us, event | category | flops | bytes accessed | tf_op | source)
XLA Modules:
  0.0 266.1 jit_solution(7309747578162263697)
XLA Ops:
  0.6 0.9 copy.11
  1.6 15.7 %gather_pt.4.cam_ref = f32[8,9,16,128]{3,2,1,0:T(8,128)S(1)} custom-call(f32[9,16,128]{2,1,0:T(8,128)S(1)} %slice.107.x_ref), custom_call_target="tpu_custom_call" | custom-call | tf_op jit(solution)/shard_map/gather_pt/pallas_call | solution.py:303
  18.7 13.0 %forward_first.1 = (f32[4,9,16,1024]{3,2,1,0:T(8,128)}, f32[2,64,4096]{2,1,0:T(8,128)}) custom-call(s32[64]{0:T(128)} %bitcast.227, s32[64]{0:T(128)} %bitcast.231, s32[1]{0:T(128)} %bitcast.196.count, f32[8,9,16,128]{3,2,1,0:T(8,128)} %copy-done, s32[64,4096]{1,0:T(8,128)} %bitcast.208, bf16[18,64,4096]{2,1,0:T(8,128)(2,1)} %bitcast.200, ...), custom_call_target="tpu_custom_call" | custom-call | tf_op jit(solution)/shard_map/forward_first/pallas_call | solution.py:214
  31.7 1.7 copy-done.6
  33.4 30.0 %scatter_cam.2 = f32[9,16,1024]{2,1,0:T(8,128)S(1)} custom-call(f32[4,9,16,1024]{3,2,1,0:T(8,128)S(1)} %copy-done.6), custom_call_target="tpu_custom_call" | custom-call | tf_op jit(solution)/shard_map/scatter_cam/pallas_call | solution.py:303
  63.7 11.0 %gather_cam.5.z_ref = f32[4,3,16,1024]{3,2,1,0:T(8,128)S(1)} custom-call(f32[3,16,1024]{2,1,0:T(8,128)S(1)} %pad_maximum_fusion.x_ref), custom_call_target="tpu_custom_call" | custom-call | tf_op jit(solution)/shard_map/gather_cam/pallas_call | solution.py:303
  75.5 17.0 %backward.2.x_ref = f32[8,9,16,128]{3,2,1,0:T(8,128)} custom-call(s32[64]{0:T(128)} %bitcast.228, s32[64]{0:T(128)} %bitcast.232, s32[1]{0:T(128)} %bitcast.197.count, f32[4,3,16,1024]{3,2,1,0:T(8,128)} %copy-done.3, f32[2,64,4096]{2,1,0:T(8,128)} %get-tuple-element.7.proj_ref, s32[64,4096]{1,0:T(8,128)} %bitcast.209, bf16[18,64,4096]{2,1,0:T(8,128)(2,1)} %bitcast.201, ...), custom_call_target="tpu_custom_call" | custom-call | tf_op jit(solution)/shard_map/backward/pallas_call | solution.py:236
  92.6 1.1 copy-done.5
  93.6 29.9 %scatter_pt.2 = f32[9,16,128]{2,1,0:T(8,128)S(1)} custom-call(f32[8,9,16,128]{3,2,1,0:T(8,128)S(1)} %copy-done.5), custom_call_target="tpu_custom_call" | custom-call | tf_op jit(solution)/shard_map/scatter_pt/pallas_call | solution.py:303
  124.8 9.5 %gather_pt.5 = f32[8,1,8,128]{3,2,1,0:T(8,128)S(1)} custom-call(f32[1,8,128]{2,1,0:T(8,128)S(1)} %broadcast_in_dim.10.x_ref), custom_call_target="tpu_custom_call" | custom-call | tf_op jit(solution)/shard_map/gather_pt/pallas_call | solution.py:303
  135.8 1.4 pad_maximum_fusion.4
  137.3 3.7 %gather_cam.6 = f32[4,2,8,128]{3,2,1,0:T(8,128)S(1)} custom-call(f32[2,8,128]{2,1,0:T(8,128)S(1)} %broadcast_in_dim.11.x_ref), custom_call_target="tpu_custom_call" | custom-call | tf_op jit(solution)/shard_map/gather_cam/pallas_call | solution.py:303
  143.2 14.1 %gather_pt.6 = f32[8,9,16,128]{3,2,1,0:T(8,128)S(1)} custom-call(f32[9,16,128]{2,1,0:T(8,128)S(1)} %multiply_subtract_fusion.1.x_ref), custom_call_target="tpu_custom_call" | custom-call | tf_op jit(solution)/shard_map/gather_pt/pallas_call | solution.py:303
  158.7 3.7 %gather_cam.7 = f32[4,2,8,128]{3,2,1,0:T(8,128)S(1)} custom-call(f32[2,8,128]{2,1,0:T(8,128)S(1)} %broadcast_in_dim.12.x_ref), custom_call_target="tpu_custom_call" | custom-call | tf_op jit(solution)/shard_map/gather_cam/pallas_call | solution.py:303
  164.2 11.4 %forward_next.1 = (f32[4,3,16,1024]{3,2,1,0:T(8,128)}, f32[2,64,4096]{2,1,0:T(8,128)}) custom-call(s32[64]{0:T(128)} %bitcast.229, s32[64]{0:T(128)} %bitcast.233, s32[1]{0:T(128)} %bitcast.198.count, f32[8,9,16,128]{3,2,1,0:T(8,128)} %multiply_add_fusion.cam_ref, s32[64,4096]{1,0:T(8,128)} %bitcast.210, bf16[18,64,4096]{2,1,0:T(8,128)(2,1)} %bitcast.202, ...), custom_call_target="tpu_custom_call" | custom-call | tf_op jit(solution)/shard_map/forward_next/pallas_call | solution.py:214
  175.6 1.1 copy-done.7
  176.8 11.4 %scatter_cam.3 = f32[3,16,1024]{2,1,0:T(8,128)S(1)} custom-call(f32[4,3,16,1024]{3,2,1,0:T(8,128)S(1)} %copy-done.7), custom_call_target="tpu_custom_call" | custom-call | tf_op jit(solution)/shard_map/scatter_cam/pallas_call | solution.py:303
  188.2 11.0 %gather_cam.8.z_ref = f32[4,3,16,1024]{3,2,1,0:T(8,128)S(1)} custom-call(f32[3,16,1024]{2,1,0:T(8,128)S(1)} %pad_maximum_fusion.1.x_ref), custom_call_target="tpu_custom_call" | custom-call | tf_op jit(solution)/shard_map/gather_cam/pallas_call | solution.py:303
  199.2 0.9 copy-done.2
  200.1 16.9 %backward.3.x_ref = f32[8,9,16,128]{3,2,1,0:T(8,128)} custom-call(s32[64]{0:T(128)} %bitcast.230, s32[64]{0:T(128)} %bitcast.234, s32[1]{0:T(128)} %bitcast.199.count, f32[4,3,16,1024]{3,2,1,0:T(8,128)} %copy-done.2, f32[2,64,4096]{2,1,0:T(8,128)} %get-tuple-element.9.proj_ref, s32[64,4096]{1,0:T(8,128)} %bitcast.211, bf16[18,64,4096]{2,1,0:T(8,128)(2,1)} %bitcast.203, ...), custom_call_target="tpu_custom_call" | custom-call | tf_op jit(solution)/shard_map/backward/pallas_call | solution.py:236
  217.0 1.1 copy-done.4
  218.0 30.5 %scatter_pt.3 = f32[9,16,128]{2,1,0:T(8,128)S(1)} custom-call(f32[8,9,16,128]{3,2,1,0:T(8,128)S(1)} %copy-done.4), custom_call_target="tpu_custom_call" | custom-call | tf_op jit(solution)/shard_map/scatter_pt/pallas_call | solution.py:303
  249.8 9.5 %gather_pt.7 = f32[8,1,8,128]{3,2,1,0:T(8,128)S(1)} custom-call(f32[1,8,128]{2,1,0:T(8,128)S(1)} %broadcast_in_dim.13.x_ref), custom_call_target="tpu_custom_call" | custom-call | tf_op jit(solution)/shard_map/gather_pt/pallas_call | solution.py:303
  260.7 3.7 %gather_cam.9 = f32[4,2,8,128]{3,2,1,0:T(8,128)S(1)} custom-call(f32[2,8,128]{2,1,0:T(8,128)S(1)} %broadcast_in_dim.14.x_ref), custom_call_target="tpu_custom_call" | custom-call | tf_op jit(solution)/shard_map/gather_cam/pallas_call | solution.py:303
  (49 shorter events, 12.3 us)
Async XLA Ops:
  17.3 0.8 copy-start
  31.7 1.7 copy-start.6
  33.4 30.0 %copy-start.8 = (f32[65536]{0:T(1024)S(1)}, f32[65536]{0:T(1024)}, u32[]{:S(2)}) copy-start(f32[65536]{0:T(1024)} %param.11) | copy-start | bytes 786436
  74.7 0.9 copy-start.3
  75.5 48.0 %copy-start.9 = (f32[9,2048]{1,0:T(8,128)S(1)}, f32[9,2048]{1,0:T(8,128)}, u32[]{:S(2)}) copy-start(f32[9,2048]{1,0:T(8,128)} %param.10) | copy-start | bytes 221188
  75.5 59.5 %copy-start.1 = (f32[8,9,16,128]{3,2,1,0:T(8,128)S(1)}, f32[8,9,16,128]{3,2,1,0:T(8,128)}, u32[]{:S(2)}) copy-start(f32[8,9,16,128]{3,2,1,0:T(8,128)} %copy-done) | copy-start | bytes 1769476
  92.6 1.1 copy-start.5
  175.6 1.1 copy-start.7
  199.2 0.9 copy-start.2
  217.0 1.1 copy-start.4
